TPU v7x, 32 devices: a whole 2x2x4 slice. The times are simulated.
32 devices in a mesh: row: 8 (over z, y), col: 4 (over x, core).
Axes of the slice: x: 2, y: 2, z: 4, core: 2. Of those that a mesh axis runs over, the one named last changes fastest.
Arguments:
- amplitudes: float32 [64, 2, 640], P('row', None, 'col'), may hold values from -6 to 6
- integrals: float32 [2, 640, 640, 640], P(None, 'col', 'row'), may hold values from -0.5 to 0.5
- virt_irrep: int32 [640], replicated, may hold values from 0 to 7
- pair_irrep: int32 [64], replicated, may hold values from 0 to 7
- tile_mask: int32 [8, 8], replicated, may hold values 0 or 1
Outputs:
- residual: float32 [64, 640, 640], P('col', 'row')
All inputs are finite; a program needn't handle non-finite values.
Results may differ from a plain program's by a relative error of at most 0.000071.
Values sent between devices are 32-bit elements; how exact they have to be, the bound alone decides.
A program may use at most 192 MiB of HBM per device.

v0:
```python
import jax
import jax.numpy as jnp
from jax import lax
from jax.sharding import PartitionSpec as P


def reduce_pairs(partial_sums):
    return lax.psum_scatter(partial_sums, "col", scatter_dimension=0, tiled=True)


def mirror_after(owned):
    swapped = lax.all_to_all(owned, "row", split_axis=2, concat_axis=1, tiled=True)
    return owned - jnp.transpose(swapped, (0, 2, 1))


def mask_slab(amps, c_labels, d_labels, pair_irrep, tile_mask):
    labels_range = jnp.arange(tile_mask.shape[0], dtype=jnp.int32)
    c_onehot = (c_labels[:, None] == labels_range[None, :]).astype(jnp.float32)
    d_onehot = (d_labels[:, None] == labels_range[None, :]).astype(jnp.float32)
    tile_float = tile_mask.astype(jnp.float32)
    screen = jnp.dot(
        jnp.dot(
            c_onehot,
            tile_float,
            precision=lax.Precision.HIGHEST,
            preferred_element_type=jnp.float32,
        ),
        d_onehot.T,
        precision=lax.Precision.HIGHEST,
        preferred_element_type=jnp.float32,
    )
    allowed = (
        jnp.bitwise_xor(c_labels[:, None], d_labels[None, :])[None, :, :]
        == pair_irrep[:, None, None]
    )
    return amps * screen[None, :, :] * allowed.astype(jnp.float32)


def local(amplitudes, integrals, virt_irrep, pair_irrep, tile_mask):
    slab_width = amplitudes.shape[1]
    d_width = integrals.shape[1]
    a_width = integrals.shape[2]
    full_width = integrals.shape[3]
    row_index = lax.axis_index("row")
    col_index = lax.axis_index("col")
    gathered = lax.all_gather(amplitudes, "row", axis=0, tiled=True)
    pair_count = gathered.shape[0]
    c_labels = virt_irrep[:slab_width]
    d_labels = lax.dynamic_slice_in_dim(virt_irrep, col_index * d_width, d_width)
    masked = mask_slab(gathered, c_labels, d_labels, pair_irrep, tile_mask)
    partial_sums = jnp.dot(
        masked.reshape(pair_count, slab_width * d_width),
        integrals.reshape(slab_width * d_width, a_width * full_width),
        precision=lax.Precision.HIGHEST,
        preferred_element_type=jnp.float32,
    ).reshape(pair_count, a_width, full_width)
    mirrored = mirror_after(reduce_pairs(partial_sums))
    own_pairs = mirrored.shape[0]
    a_labels = lax.dynamic_slice_in_dim(virt_irrep, row_index * a_width, a_width)
    pair_labels = lax.dynamic_slice_in_dim(pair_irrep, col_index * own_pairs, own_pairs)
    kept_mask = (
        jnp.bitwise_xor(a_labels[:, None], virt_irrep[None, :])[None, :, :]
        == pair_labels[:, None, None]
    )
    return mirrored * kept_mask.astype(jnp.float32)


def solution(mesh):
    in_specs = (P("row", None, "col"), P(None, "col", "row", None), P(), P(), P())
    out_specs = P("col", "row", None)
    return jax.shard_map(local, mesh=mesh, in_specs=in_specs, out_specs=out_specs, check_vma=False)
```

profile of v0, /device:TPU:0, one launch (start us, length us, event | category | flops | bytes accessed | tf_op | source)
XLA Modules:
  0.0 375.9 jit_solution(2555133089651261318)
XLA Ops:
  6.5 0.0 reduce-scatter.2.cloned.1.call-start
  6.5 0.7 slice.3
  7.2 0.8 dynamic_slice.11
  8.0 0.9 fusion.6
  8.9 0.1 broadcast_xor_fusion.1
  8.9 0.2 fusion.4
  9.1 32.6 %all_gather.3 = f32[64,2,160]{2,1,0:T(2,128)S(1)} all-gather(f32[8,2,160]{2,1,0:T(2,128)} %param.5), channel_id=1, replica_groups=mesh['row'=8,'col'=4] {'row'}, dimensions={0}, use_global_device_ids=true | all-gather | bytes 92160 | tf_op jit(solution)/shard_map/all_gather | solution.py:46
  41.7 0.8 compare_select_fusion
  42.5 0.1 reshape.68
  42.7 79.4 %fusion = f32[64,80,640]{2,0,1:T(8,128)} fusion(f32[64,320,1]{1,0,2:T(8,128)S(1)} %reshape.68, f32[40,8,80,640]{3,2,1,0:T(8,128)} %bitcast.26), kind=kOutput, calls=%fused_computation | convolution fusion | flops 12582912000 | bytes 78725120 | tf_op jit(solution)/shard_map/dot_general | solution.py:51
  122.1 0.0 reduce-scatter.2.cloned.1.call-update
  122.2 101.4 %reduce-scatter.2.cloned.1.call-done = f32[16,80,640]{2,0,1:T(8,128)} async-done(((f32[64,80,640]{2,0,1:T(8,128)}), f32[16,80,640]{2,0,1:T(8,128)}) %reduce-scatter.2.cloned.1.call-update) | async-done | bytes 3276816 | tf_op jit(solution)/shard_map/reduce_scatter | solution.py:8
  223.6 5.6 %copy.16 = f32[16,80,640]{1,0,2:T(8,128)} copy(f32[16,80,640]{2,0,1:T(8,128)} %reduce-scatter.2.cloned.1.call-done) | data formatting | bytes 6553600 | tf_op jit(solution)/shard_map/reduce_scatter | solution.py:8
  229.2 0.0 copy-start.2
  229.2 0.0 copy-start.1
  229.2 5.6 %all-to-all-start = ((f32[16,80,640]{1,0,2:T(8,128)}), f32[16,80,640]{1,0,2:T(8,128)}, u32[]{:S(2)}, u32[]{:S(2)}) async-start(f32[16,80,640]{1,0,2:T(8,128)} %copy.16), calls=%async_computation.1 | async-start | bytes 10485760 | tf_op jit(solution)/shard_map/all_to_all | solution.py:12
  234.8 0.0 copy-done.2
  234.9 0.1 dynamic_slice.10
  234.9 0.0 copy-done.1
  234.9 0.1 dynamic_slice.9
  235.0 0.1 broadcast_xor_fusion
  235.1 115.3 %all-to-all-done = f32[16,80,640]{1,0,2:T(8,128)} async-done(((f32[16,80,640]{1,0,2:T(8,128)}), f32[16,80,640]{1,0,2:T(8,128)}, u32[]{:S(2)}, u32[]{:S(2)}) %all-to-all-start) | async-done | bytes 3276832 | tf_op jit(solution)/shard_map/all_to_all | solution.py:12
  350.4 7.9 %copy.29 = f32[16,80,8,80]{1,2,0,3:T(8,128)} copy(f32[16,80,8,80]{1,0,3,2:T(8,128)} %bitcast.1) | data formatting | bytes 6553600 | tf_op jit(solution)/shard_map/all_to_all | solution.py:12
  358.3 0.0 copy-start
  358.3 5.5 %all_to_all.16 = f32[16,640,80]{1,0,2:T(8,128)} reshape(f32[16,8,80,80]{2,1,0,3:T(8,128)} %bitcast.27) | data formatting | bytes 6553600 | tf_op jit(solution)/shard_map/all_to_all | solution.py:12
  363.8 0.0 copy-done
  363.8 2.5 fusion.3
  366.4 2.7 copy.18
Async XLA Ops:
  6.5 217.0 %reduce-scatter.2.cloned.1.call-start = ((), (), s32[]{:S(2)}) async-start(), calls=%async_computation.2 | async-start | bytes 16384000 | tf_op jit(solution)/shard_map/reduce_scatter | solution.py:8
  229.2 5.6 %copy-start.2 = (s32[64]{0:T(128)S(1)}, s32[64]{0:T(128)}, u32[]{:S(2)}) copy-start(s32[64]{0:T(128)} %param.8) | copy-start | bytes 772
  229.2 5.7 %copy-start.1 = (s32[640]{0:T(1024)S(1)}, s32[640]{0:T(1024)}, u32[]{:S(2)}) copy-start(s32[640]{0:T(1024)} %param.7) | copy-start | bytes 7684
  229.2 121.2 %all-to-all-start = ((f32[16,80,640]{1,0,2:T(8,128)}), f32[16,80,640]{1,0,2:T(8,128)}, u32[]{:S(2)}, u32[]{:S(2)}) async-start(f32[16,80,640]{1,0,2:T(8,128)} %copy.16), calls=%async_computation.1 | async-start | bytes 10485760 | tf_op jit(solution)/shard_map/all_to_all | solution.py:12
  358.3 5.5 %copy-start = (f32[16,80,640]{2,0,1:T(8,128)S(1)}, f32[16,80,640]{2,0,1:T(8,128)}, u32[]{:S(2)}) copy-start(f32[16,80,640]{2,0,1:T(8,128)} %reduce-scatter.2.cloned.1.call-done) | copy-start | bytes 9830404
Sparse Core Ops, SparseCore 0:
  122.3 101.2 reduce-scatter.1
where the time goes:
time: 376 us
  waiting for transfers between devices  217 us (58%)
  matrix products  80.5 us (21%)
  blocking collectives  32.6 us (9%)
  local copies, waits for them, and re-layouts  23.5 us (6%)
  between operations  13.4 us (4%)
  starting transfers between devices  5.64 us (2%)
    all_to_all x1, waiting for transfers between devices, mirror_after(): lax.all_to_all(owned, 'row', split_axis=2, concat_axis=1, tiled=True)  115 us
    reduce_scatter x1, waiting for transfers between devices, reduce_pairs(): lax.psum_scatter(partial_sums, 'col', scatter_dimension=0, tiled=True)  101 us
    dot_general x1, matrix products, local(): jnp.dot(masked.reshape(pair_count, slab_width * d_width), integrals.resha...  79.4 us
    all_gather x1, blocking collectives, local(): gathered = lax.all_gather(amplitudes, 'row', axis=0, tiled=True)  32.6 us
    all_to_all x2, local copies, waits for them, and re-layouts, mirror_after(): lax.all_to_all(owned, 'row', split_axis=2, concat_axis=1, tiled=True)  13.4 us
  transfers between devices with their start and end apart: 2, of which 2 were waited for; matrix products, arithmetic and copies ran while one was open for 0% of the time, Pallas kernels for 0%

commit v1 on v0

--- a/solution.py
+++ b/solution.py
@@ -1,7 +1,41 @@
+import functools
 import jax
 import jax.numpy as jnp
 from jax import lax
 from jax.sharding import PartitionSpec as P
+from jax.lax import axis_index, axis_size, ppermute
+
+
+def spread_slabs(payload, array_dim):
+    current_arr = list(payload.shape[1:])
+    current_arr[array_dim] *= payload.shape[0]
+    plain = jnp.moveaxis(payload, 0, array_dim).reshape(current_arr)
+    return plain
+
+
+def store_the_grid(frame_in, mesh_ax):
+    left_arr = axis_index(mesh_ax)
+    y2 = axis_size(mesh_ax)
+    a_now, before = (y2, left_arr)
+    met_up, tile_out = (frame_in[None], 1)
+    while tile_out < a_now:
+        y1 = tuple(((i, i ^ tile_out) for i in range(a_now)))
+        u_next = ppermute(met_up, mesh_ax, perm=y1)
+        z1 = before & tile_out == 0
+        heard = jnp.where(z1, met_up, u_next)
+        y_new = jnp.where(z1, u_next, met_up)
+        met_up = jnp.concatenate([heard, y_new])
+        tile_out *= 2
+    return met_up
+
+
+def arrange_cycles(xx, x_in, dim_k):
+    res = store_the_grid(xx, x_in)
+    back = spread_slabs(res, dim_k)
+    return back
+
+
+proceed_slot_on_mesh = functools.partial(arrange_cycles, x_in="row", dim_k=0)
 
 
 def reduce_pairs(partial_sums):
@@ -43,7 +77,7 @@
     full_width = integrals.shape[3]
     row_index = lax.axis_index("row")
     col_index = lax.axis_index("col")
-    gathered = lax.all_gather(amplitudes, "row", axis=0, tiled=True)
+    gathered = proceed_slot_on_mesh(amplitudes)
     pair_count = gathered.shape[0]
     c_labels = virt_irrep[:slab_width]
     d_labels = lax.dynamic_slice_in_dim(virt_irrep, col_index * d_width, d_width)

time: 376 us -> 357 us (0.949)
  blocking collectives: 32.6 us -> 0 us
  starting transfers between devices: 5.64 us -> 13.1 us
  waiting for transfers between devices: 217 us -> 222 us
    all_gather x1 -> x0, blocking collectives: 32.6 us -> none  [local(): gathered = lax.all_gather(amplitudes, 'row', axis=0, tiled=True)]
    ppermute x0 -> x3, starting transfers between devices: none -> 7.49 us  [store_the_grid(): u_next = ppermute(met_up, mesh_ax, perm=y1)]
  transfers between devices with their start and end apart: 2 -> 5, of which waited for: 2 -> 4; matrix products, arithmetic and copies ran while one was open for 0% -> 1% of each run, Pallas kernels for 0% -> 0%
where the time goes in v1:
time: 357 us
  waiting for transfers between devices  222 us (62%)
  matrix products  80.6 us (23%)
  local copies, waits for them, and re-layouts  24.2 us (7%)
  between operations  13.5 us (4%)
  starting transfers between devices  13.1 us (4%)
  other arithmetic  3.69 us (1%)
    all_to_all x1, waiting for transfers between devices, mirror_after(): lax.all_to_all(owned, 'row', split_axis=2, concat_axis=1, tiled=True)  115 us
    reduce_scatter x1, waiting for transfers between devices, reduce_pairs(): lax.psum_scatter(partial_sums, 'col', scatter_dimension=0, tiled=True)  103 us
    dot_general x1, matrix products, local(): jnp.dot(masked.reshape(pair_count, slab_width * d_width), integrals.resha...  79.6 us
    all_to_all x2, local copies, waits for them, and re-layouts, mirror_after(): lax.all_to_all(owned, 'row', split_axis=2, concat_axis=1, tiled=True)  13.4 us
    ppermute x3, starting transfers between devices, store_the_grid(): u_next = ppermute(met_up, mesh_ax, perm=y1)  7.49 us
  transfers between devices with their start and end apart: 5, of which 4 were waited for; matrix products, arithmetic and copies ran while one was open for 1% of the time, Pallas kernels for 0%

profile of v1, /device:TPU:0, one launch (start us, length us, event | category | flops | bytes accessed | tf_op | source)
XLA Modules:
  0.0 356.7 jit_solution(8757597381620441023)
XLA Ops:
  6.5 0.0 reduce-scatter.2.cloned.1.call-start
  6.5 3.0 collective-permute-start
  9.5 0.7 slice.3
  10.2 0.9 fusion.6
  11.1 0.8 dynamic_slice.11
  11.9 0.0 collective-permute-done
  11.9 0.7 broadcast_select_fusion.5
  12.6 1.7 collective-permute-start.1
  14.4 0.2 fusion.4
  14.6 2.0 collective-permute-done.1
  16.7 2.8 collective-permute-start.2
  19.4 0.1 broadcast_xor_fusion.1
  19.5 0.7 eq.75
  20.2 1.7 collective-permute-done.2
  21.9 0.1 broadcast_select_fusion.1
  22.0 0.1 compare_select_fusion
  22.1 0.1 reshape.150
  22.3 79.6 %fusion = f32[64,80,640]{2,0,1:T(8,128)} fusion(f32[64,320,1]{1,0,2:T(8,128)S(1)} %reshape.150, f32[40,8,80,640]{3,2,1,0:T(8,128)} %bitcast.29), kind=kOutput, calls=%fused_computation | convolution fusion | flops 12582912000 | bytes 78725120 | tf_op jit(solution)/shard_map/dot_general | solution.py:85
  101.8 0.0 reduce-scatter.2.cloned.1.call-update
  101.9 102.5 %reduce-scatter.2.cloned.1.call-done = f32[16,80,640]{2,0,1:T(8,128)} async-done(((f32[64,80,640]{2,0,1:T(8,128)}), f32[16,80,640]{2,0,1:T(8,128)}) %reduce-scatter.2.cloned.1.call-update) | async-done | bytes 3276816 | tf_op jit(solution)/shard_map/reduce_scatter | solution.py:42
  204.4 5.6 %copy.16 = f32[16,80,640]{1,0,2:T(8,128)} copy(f32[16,80,640]{2,0,1:T(8,128)} %reduce-scatter.2.cloned.1.call-done) | data formatting | bytes 6553600 | tf_op jit(solution)/shard_map/reduce_scatter | solution.py:42
  210.0 5.6 %all-to-all-start = ((f32[16,80,640]{1,0,2:T(8,128)}), f32[16,80,640]{1,0,2:T(8,128)}, u32[]{:S(2)}, u32[]{:S(2)}) async-start(f32[16,80,640]{1,0,2:T(8,128)} %copy.16), calls=%async_computation.1 | async-start | bytes 10485760 | tf_op jit(solution)/shard_map/all_to_all | solution.py:46
  215.6 0.0 copy-done.1
  215.6 0.1 dynamic_slice.9
  215.7 0.0 copy-done.2
  215.7 0.1 dynamic_slice.10
  215.8 0.1 broadcast_xor_fusion
  215.9 115.4 %all-to-all-done = f32[16,80,640]{1,0,2:T(8,128)} async-done(((f32[16,80,640]{1,0,2:T(8,128)}), f32[16,80,640]{1,0,2:T(8,128)}, u32[]{:S(2)}, u32[]{:S(2)}) %all-to-all-start) | async-done | bytes 3276832 | tf_op jit(solution)/shard_map/all_to_all | solution.py:46
  331.2 7.9 %copy.29 = f32[16,80,8,80]{1,2,0,3:T(8,128)} copy(f32[16,80,8,80]{1,0,3,2:T(8,128)} %bitcast.2) | data formatting | bytes 6553600 | tf_op jit(solution)/shard_map/all_to_all | solution.py:46
  339.1 5.5 %all_to_all.16 = f32[16,640,80]{1,0,2:T(8,128)} reshape(f32[16,8,80,80]{2,1,0,3:T(8,128)} %bitcast.30) | data formatting | bytes 6553600 | tf_op jit(solution)/shard_map/all_to_all | solution.py:46
  344.6 2.5 fusion.3
  347.2 2.7 copy.18
  (7 shorter events, 0.1 us)
Async XLA Ops:
  6.5 197.8 %reduce-scatter.2.cloned.1.call-start = ((), (), s32[]{:S(2)}) async-start(), calls=%async_computation.2 | async-start | bytes 16384000 | tf_op jit(solution)/shard_map/reduce_scatter | solution.py:42
  6.5 5.3 %collective-permute-start = (f32[1,8,2,160]{3,2,1,0:T(2,128)}, f32[1,8,2,160]{3,2,1,0:T(2,128)S(1)}, u32[]{:S(2)}, u32[]{:S(2)}) collective-permute-start(f32[1,8,2,160]{3,2,1,0:T(2,128)} %bitcast.31), channel_id=1, source_target_pairs={{0,4},{4,0},{8,12},{12,8},{16,20},{20,16},{24,28},{28,24},{1,5},{5... | collective-permute-start | bytes 30728 | tf_op jit(solution)/shard_map/ppermute | solution.py:23
  12.6 4.0 %collective-permute-start.1 = (f32[2,8,2,160]{3,2,1,0:T(2,128)S(1)}, f32[2,8,2,160]{3,2,1,0:T(2,128)S(1)}, u32[]{:S(2)}, u32[]{:S(2)}) collective-permute-start(f32[2,8,2,160]{3,2,1,0:T(2,128)S(1)} %pad_maximum_fusion.1), channel_id=1, source_target_pairs={{0,8},{4,12},{8,0},{12,4},{16,24},{20,28},{24,16},{28,20},{1,9},{5... | collective-permute-start | bytes 61448 | tf_op jit(solution)/shard_map/ppermute | solution.py:23
  16.7 5.2 %collective-permute-start.2 = (f32[4,8,2,160]{3,2,1,0:T(2,128)S(1)}, f32[4,8,2,160]{3,2,1,0:T(2,128)S(1)}, u32[]{:S(2)}, u32[]{:S(2)}) collective-permute-start(f32[4,8,2,160]{3,2,1,0:T(2,128)S(1)} %pad_maximum_fusion), channel_id=1, source_target_pairs={{0,16},{4,20},{8,24},{12,28},{16,0},{20,4},{24,8},{28,12},{1,17},{... | collective-permute-start | bytes 122888 | tf_op jit(solution)/shard_map/ppermute | solution.py:23
  210.0 5.6 %copy-start.1 = (s32[640]{0:T(1024)S(1)}, s32[640]{0:T(1024)}, u32[]{:S(2)}) copy-start(s32[640]{0:T(1024)} %param.7) | copy-start | bytes 7684
  210.0 5.7 %copy-start.2 = (s32[64]{0:T(128)S(1)}, s32[64]{0:T(128)}, u32[]{:S(2)}) copy-start(s32[64]{0:T(128)} %param.8) | copy-start | bytes 772
  210.0 121.2 %all-to-all-start = ((f32[16,80,640]{1,0,2:T(8,128)}), f32[16,80,640]{1,0,2:T(8,128)}, u32[]{:S(2)}, u32[]{:S(2)}) async-start(f32[16,80,640]{1,0,2:T(8,128)} %copy.16), calls=%async_computation.1 | async-start | bytes 10485760 | tf_op jit(solution)/shard_map/all_to_all | solution.py:46
  339.1 5.5 %copy-start = (f32[16,80,640]{2,0,1:T(8,128)S(1)}, f32[16,80,640]{2,0,1:T(8,128)}, u32[]{:S(2)}) copy-start(f32[16,80,640]{2,0,1:T(8,128)} %reduce-scatter.2.cloned.1.call-done) | copy-start | bytes 9830404
Sparse Core Ops, SparseCore 0:
  102.0 102.3 reduce-scatter.1
